TPU v7x, 32 devices: a whole 2x2x4 slice. The times are simulated.
32 devices in a mesh: groups: 2 (over y), seq: 4 (over z), dp: 2 (over x), mp: 2 (over core).
Axes of the slice: x: 2, y: 2, z: 4, core: 2. Of those that a mesh axis runs over, the one named last changes fastest.
Arguments:
- tiles: bfloat16 [160, 8, 8, 768], P(('groups', 'seq', 'dp')), parts along dimension 0, may hold values from -6 to 6
- token_grad: bfloat16 [160, 8, 8, 768], P(('groups', 'seq', 'dp')), parts along dimension 0, may hold values from -1.5 to 1.5
- embed_grad: bfloat16 [2, 80, 768], P('dp', 'groups', 'seq'), parts along dimension 1, may hold values from -48 to 48
- live_tiles: int32 [16], P(('groups', 'seq', 'dp')), parts along dimension 0, may hold values from 1 to 10, 60 in all
- dw_kernel: float32 [7, 7, 768], replicated, may hold values from -0.875 to 0.875
- dw_bias: float32 [768], replicated, may hold values from -3 to 3
- ln_gain: float32 [768], replicated, may hold values from 0.1 to 1.9
- ln_bias: float32 [768], replicated, may hold values from -2 to 2
- w_up: bfloat16 [768, 2560], P('seq', 'mp'), may hold values from -0.21875 to 0.21875
- b_up: float32 [2560], P('mp'), may hold values from -3 to 3
- w_down: bfloat16 [768, 2560], P('seq', 'mp'), may hold values from -0.125 to 0.125
- layer_scale: float32 [768], replicated, may hold values from 0.3 to 1.5
Outputs:
- tile_grad: bfloat16 [160, 8, 8, 768], P(('groups', 'seq', 'dp')), parts along dimension 0
- grad_up: float32 [1536, 2560], P(('groups', 'seq'), 'mp'), parts along dimension 0
- grad_down: float32 [1536, 2560], P(('groups', 'seq'), 'mp'), parts along dimension 0
There are 2 independent parts, one for each index of `groups`. A program takes and returns all parts, laid end to end along the dimension named above; an argument that names none is the same for every part. Nothing has to cross between parts.
Inputs may be any that keep to these rules, and one draw needn't show every extreme that they name: Each loader's foreground tiles fill its slots 0 to live_tiles - 1 of 10; some loader has all 10.
All inputs are finite; a program needn't handle non-finite values. No bound on the sum of `live_tiles` on one device may be relied on, other than what follows from the above.
Results may differ from a plain program's by a relative error of at most 0.01.
Values may be sent and summed in bfloat16 or wider, within the bound.
No kernel may reach another device: no remote copies, remote signals or barrier semaphores. Data moves between devices by JAX's collectives and lax.ppermute only.
A program may use at most 64 MiB of HBM per device.

v0:
```python
import jax
import jax.numpy as jnp
from jax import lax
from jax.sharding import PartitionSpec as P

sqrt_two_pi = 0.7978845608028654
cubic_coef = 0.044715


def depthwise(values, kernel):
    reach = kernel.shape[0]
    margin = reach // 2
    height = values.shape[1]
    padded = jnp.pad(values, ((0, 0), (margin, margin), (margin, margin), (0, 0)))
    total = jnp.zeros(values.shape, jnp.float32)
    for row_off in range(reach):
        for col_off in range(reach):
            total = (
                total
                + padded[:, row_off : row_off + height, col_off : col_off + height, :]
                * kernel[row_off, col_off]
            )
    return total


def gelu_tanh(values):
    inner = sqrt_two_pi * (values + cubic_coef * values * values * values)
    return 0.5 * values * (1.0 + jnp.tanh(inner))


def gelu_slope(values):
    tangent = jnp.tanh(sqrt_two_pi * (values + cubic_coef * values * values * values))
    return 0.5 * (1.0 + tangent) + 0.5 * values * (1.0 - tangent * tangent) * sqrt_two_pi * (
        1.0 + 3.0 * cubic_coef * values * values
    )


def normalize(values):
    center = jnp.mean(values, axis=-1, keepdims=True)
    shifted = values - center
    spread = jnp.sqrt(jnp.mean(shifted * shifted, axis=-1, keepdims=True) + 1e-06)
    return (shifted / spread, spread)


def norm_backward(normed_grad, normal, spread, ln_gain):
    scaled = normed_grad * ln_gain
    return (
        scaled
        - jnp.mean(scaled, axis=-1, keepdims=True)
        - normal * jnp.mean(scaled * normal, axis=-1, keepdims=True)
    ) / spread


def on_device(
    tiles,
    token_grad,
    embed_grad,
    live_tiles,
    dw_kernel,
    dw_bias,
    ln_gain,
    ln_bias,
    w_up,
    b_up,
    w_down,
    layer_scale,
):
    count = tiles.shape[0]
    height = tiles.shape[1]
    width = tiles.shape[3]
    flipped = dw_kernel[::-1, ::-1, :]
    arrived = lax.all_to_all(embed_grad[0], "seq", split_axis=0, concat_axis=1, tiled=True)
    live = (jnp.arange(count) < live_tiles[0]).astype(jnp.float32)[:, None, None, None]
    pooled = arrived.astype(jnp.float32)[:, None, None, :] * live
    out_grad = live * token_grad.astype(jnp.float32) + pooled / (height * height)
    branch_grad = (layer_scale * out_grad).astype(jnp.bfloat16).reshape(-1, width)
    conv = depthwise(tiles.astype(jnp.float32), dw_kernel) + dw_bias
    normal, spread = normalize(conv)
    normed = (normal * ln_gain + ln_bias).astype(jnp.bfloat16)
    rows = normed.reshape(-1, width)
    full_up, full_down = (
        lax.all_gather(w_up, "seq", axis=0, tiled=True),
        lax.all_gather(w_down, "seq", axis=0, tiled=True),
    )
    hidden = jnp.dot(rows, full_up, preferred_element_type=jnp.float32) + b_up
    act = gelu_tanh(hidden).astype(jnp.bfloat16)
    act_grad = jnp.dot(branch_grad, full_down, preferred_element_type=jnp.float32)
    hidden_grad = (act_grad * gelu_slope(hidden)).astype(jnp.bfloat16)
    normed_part = lax.dot_general(
        hidden_grad, full_up, (((1,), (1,)), ((), ())), preferred_element_type=jnp.float32
    )
    part_down = lax.dot_general(
        branch_grad, act, (((0,), (0,)), ((), ())), preferred_element_type=jnp.float32
    )
    part_up = lax.dot_general(
        rows, hidden_grad, (((0,), (0,)), ((), ())), preferred_element_type=jnp.float32
    )
    up_piece, down_piece = (
        lax.psum_scatter(
            part_up.astype(jnp.bfloat16), "seq", scatter_dimension=0, tiled=True
        ).astype(jnp.float32),
        lax.psum_scatter(
            part_down.astype(jnp.bfloat16), "seq", scatter_dimension=0, tiled=True
        ).astype(jnp.float32),
    )
    grad_up, grad_down = (
        lax.psum(up_piece.astype(jnp.bfloat16), "dp").astype(jnp.float32),
        lax.psum(down_piece.astype(jnp.bfloat16), "dp").astype(jnp.float32),
    )
    normed_grad = lax.psum(normed_part.astype(jnp.bfloat16), "mp").astype(jnp.float32)
    conv_grad = norm_backward(normed_grad.reshape(conv.shape), normal, spread, ln_gain)
    tile_grad = (out_grad + depthwise(conv_grad, flipped)).astype(jnp.bfloat16)
    return (tile_grad, grad_up, grad_down)


def solution(mesh):
    return jax.shard_map(
        on_device,
        mesh=mesh,
        in_specs=(
            P(("groups", "seq", "dp"), None, None, None),
            P(("groups", "seq", "dp"), None, None, None),
            P("dp", "groups", "seq"),
            P(("groups", "seq", "dp")),
            P(),
            P(),
            P(),
            P(),
            P("seq", "mp"),
            P("mp"),
            P("seq", "mp"),
            P(),
        ),
        out_specs=(
            P(("groups", "seq", "dp"), None, None, None),
            P(("groups", "seq"), "mp"),
            P(("groups", "seq"), "mp"),
        ),
        check_vma=False,
    )
```

profile of v0, /device:TPU:0, one launch (start us, length us, event | category | flops | bytes accessed | tf_op | source)
XLA Modules:
  0.0 267.0 jit_solution(10190657379910288535)
XLA Ops:
  7.2 0.0 all-gather.5.cloned.1.call-start
  7.2 0.7 all-gather.5.cloned.1.call-update
  7.9 0.7 all_to_all.10
  8.7 0.7 reshape.223
  9.4 6.5 %all-to-all-start = ((bf16[4,2,960]{2,1,0:T(2,128)(2,1)}), bf16[4,2,960]{2,1,0:T(2,128)(2,1)S(1)}, u32[]{:S(2)}, u32[]{:S(2)}) async-start(bf16[4,2,960]{2,1,0:T(2,128)(2,1)} %reshape.223), calls=%async_computation | async-start | bytes 32768 | tf_op jit(solution)/shard_map/all_to_all | solution.py:72
  15.8 0.7 all-gather.3.cloned.1.call-update
  16.6 0.0 all-reduce.6.cloned.1.call-start
  16.6 1.1 slice_reduce_fusion.46
  17.7 1.4 slice_reduce_fusion.48
  19.1 1.4 slice_reduce_fusion.47
  20.5 0.2 convert_element_type.70
  20.7 13.0 %fusion.209 = (f32[10,8,8]{2,1,0:T(8,128)S(1)}, f32[10,8,8,768]{3,2,1,0:T(8,128)S(1)}) fusion(f32[768]{0:T(1024)S(1)} %copy-done.5, f32[768]{0:T(1024)S(1)} %get-tuple-element.50, f32[768]{0:T(1024)S(1)} %get-tuple-element.51, f32[768]{0:T(1024)S(1)} %get-tuple-element.4, f32[768]{0:T(1024)S(1)} %get-tuple-element.5, f32[768]{0:T(1024)S(1)} %get-tuple-element.6, ...), kind=kLoop, calls=%fused_computation.377 | loop fusion | flops 48659840 | bytes 4088320 | tf_op jit(solution)/shard_map/reduce_sum | solution.py:39
  34.4 0.3 multiply_reduce_fusion.2
  34.7 0.0 copy-start
  34.7 0.0 copy-start.4
  34.7 0.0 copy-done.2
  34.8 1.3 add_convert_fusion
  36.1 0.0 all-to-all-done
  36.1 0.1 reshape.224
  36.3 0.1 reshape.173
  36.4 0.1 multiply_multiply_fusion.1
  36.4 1.3 multiply_convert_fusion.1
  37.7 18.1 %all-gather.5.cloned.1.call-done = bf16[768,1280]{1,0:T(8,128)(2,1)} async-done(((bf16[192,1280]{1,0:T(8,128)(2,1)}), bf16[768,1280]{1,0:T(8,128)(2,1)}) %all-gather.5.cloned.1.call-update) | async-done | bytes 1966096 | tf_op jit(solution)/shard_map/all_gather | solution.py:82
  55.9 5.0 %convolution_add_fusion = f32[640,1280]{1,0:T(8,128)} fusion(bf16[640,768]{1,0:T(8,128)(2,1)} %bitcast.18, bf16[768,1280]{1,0:T(8,128)(2,1)} %all-gather.5.cloned.1.call-done, f32[1280]{0:T(1024)S(1)} %copy-done.7), kind=kOutput, calls=%fused_computation.99 | convolution fusion | flops 1259110400 | bytes 6231040 | tf_op jit(solution)/shard_map/dot_general | solution.py:85
  60.9 39.0 %all-gather.3.cloned.1.call-done = bf16[768,1280]{1,0:T(8,128)(2,1)} async-done(((bf16[192,1280]{1,0:T(8,128)(2,1)}), bf16[768,1280]{1,0:T(8,128)(2,1)}) %all-gather.3.cloned.1.call-update) | async-done | bytes 1966096 | tf_op jit(solution)/shard_map/all_gather | solution.py:83
  99.9 5.7 %fusion.5 = bf16[640,1280]{1,0:T(8,128)(2,1)S(1)} fusion(f32[640,1280]{1,0:T(8,128)} %convolution_add_fusion, bf16[640,768]{1,0:T(8,128)(2,1)} %bitcast.20, bf16[768,1280]{1,0:T(8,128)(2,1)} %all-gather.3.cloned.1.call-done), kind=kOutput, calls=%fused_computation.108 | convolution fusion | flops 1273856000 | bytes 7864320 | tf_op jit(solution)/shard_map/dot_general | solution.py:87
  105.6 1.2 copy-done.8
  106.8 2.4 convolution_convert_fusion.2
  109.2 0.0 all-reduce.6.cloned.1.call-update
  109.2 0.0 reduce-scatter.3.cloned.1.call-start
  109.3 4.8 %convolution_convert_fusion.1 = bf16[768,1280]{1,0:T(8,128)(2,1)} fusion(bf16[640,768]{1,0:T(8,128)(2,1)} %bitcast.19, bf16[640,1280]{1,0:T(8,128)(2,1)} %copy-done.8), kind=kOutput, calls=%fused_computation.101 | convolution fusion | flops 1259274240 | bytes 4587520 | tf_op jit(solution)/shard_map/dot_general | solution.py:95
  114.1 0.0 reduce-scatter.3.cloned.1.call-update
  114.1 0.2 reduce-scatter.5.cloned.1.call-start
  114.3 5.5 %convolution_convert_fusion = bf16[768,1280]{1,0:T(8,128)(2,1)} fusion(bf16[640,768]{1,0:T(8,128)(2,1)} %bitcast.21, f32[640,1280]{1,0:T(8,128)} %convolution_add_fusion), kind=kOutput, calls=%fused_computation.100 | convolution fusion | flops 1266647040 | bytes 6225920 | tf_op jit(solution)/shard_map/dot_general | solution.py:92
  119.9 0.0 reduce-scatter.5.cloned.1.call-update
  119.9 0.0 all-reduce.8.cloned.1.call-start
  119.9 7.8 %all-reduce.6.cloned.1.call-done = bf16[640,768]{1,0:T(8,128)(2,1)} async-done(((bf16[640,768]{1,0:T(8,128)(2,1)}), bf16[640,768]{1,0:T(8,128)(2,1)}) %all-reduce.6.cloned.1.call-update) | async-done | bytes 983056 | tf_op jit(solution)/shard_map/psum | solution.py:110
  127.7 1.5 multiply_reduce_fusion.1
  129.2 0.1 div.41
  129.3 1.8 multiply_reduce_fusion
  131.1 1.9 subtract_divide_fusion
  133.0 39.7 %reduce-scatter.3.cloned.1.call-done = bf16[192,1280]{1,0:T(8,128)(2,1)} async-done(((bf16[768,1280]{1,0:T(8,128)(2,1)}), bf16[192,1280]{1,0:T(8,128)(2,1)}) %reduce-scatter.3.cloned.1.call-update) | async-done | bytes 491536 | tf_op jit(solution)/shard_map/reduce_scatter | solution.py:99
  172.7 43.0 %reduce-scatter.5.cloned.1.call-done = bf16[192,1280]{1,0:T(8,128)(2,1)} async-done(((bf16[768,1280]{1,0:T(8,128)(2,1)}), bf16[192,1280]{1,0:T(8,128)(2,1)}) %reduce-scatter.5.cloned.1.call-update) | async-done | bytes 491536 | tf_op jit(solution)/shard_map/reduce_scatter | solution.py:102
  215.6 0.0 all-reduce.8.cloned.1.call-update
  215.7 38.3 %fusion.200 = bf16[10,8,8,768]{3,2,1,0:T(8,128)(2,1)} fusion(f32[10,8,8,768]{3,2,1,0:T(8,128)} %subtract_divide_fusion, bf16[10,8,8,768]{3,2,1,0:T(8,128)(2,1)S(1)} %copy-done, f32[768]{0:T(1024)S(1)} %get-tuple-element.50, f32[768]{0:T(1024)S(1)} %get-tuple-element.51, f32[768]{0:T(1024)S(1)} %get-tuple-element.4, f32[768]{0:T(1024)S(1)} %get-tuple-element.5, ...), kind=kLoop, calls=%fused_computation.310 | loop fusion | flops 50135040 | bytes 4113448 | tf_op jit(solution)/shard_map/convert_element_type | solution.py:112
  254.0 2.1 all-reduce.8.cloned.1.call-done
  256.1 2.0 convert_element_type.77
  258.1 2.0 convert_element_type.80
  (22 shorter events, 0.1 us)
Async XLA Ops:
  7.2 13.3 %copy-start.1 = (bf16[10,8,8,768]{3,2,1,0:T(8,128)(2,1)S(1)}, bf16[10,8,8,768]{3,2,1,0:T(8,128)(2,1)}, u32[]{:S(2)}) copy-start(bf16[10,8,8,768]{3,2,1,0:T(8,128)(2,1)} %param.12) | copy-start | bytes 2949124
  7.2 48.7 %all-gather.5.cloned.1.call-start = ((), (), s32[]{:S(2)}) async-start(), calls=%async_computation.4 | async-start | bytes 2457600 | tf_op jit(solution)/shard_map/all_gather | solution.py:82
  9.4 11.3 %copy-start.5 = (f32[768]{0:T(1024)S(1)}, f32[768]{0:T(1024)}, u32[]{:S(2)}) copy-start(f32[768]{0:T(1024)} %param.17) | copy-start | bytes 9220
  9.4 26.7 %all-to-all-start = ((bf16[4,2,960]{2,1,0:T(2,128)(2,1)}), bf16[4,2,960]{2,1,0:T(2,128)(2,1)S(1)}, u32[]{:S(2)}, u32[]{:S(2)}) async-start(bf16[4,2,960]{2,1,0:T(2,128)(2,1)} %reshape.223), calls=%async_computation | async-start | bytes 32768 | tf_op jit(solution)/shard_map/all_to_all | solution.py:72
  15.8 84.0 %all-gather.3.cloned.1.call-start = ((), (), s32[]{:S(2)}) async-start(), calls=%async_computation.3 | async-start | bytes 2457600 | tf_op jit(solution)/shard_map/all_gather | solution.py:83
  16.6 111.2 %all-reduce.6.cloned.1.call-start = ((), (), s32[]{:S(2)}) async-start(), calls=%async_computation.5 | async-start | bytes 1966080 | tf_op jit(solution)/shard_map/psum | solution.py:110
  33.6 1.1 copy-start.2
  33.7 1.1 copy-start.3
  34.7 1.7 copy-start
  34.7 1.7 copy-start.4
  36.1 19.8 %copy-start.7 = (f32[1280]{0:T(1024)S(1)}, f32[1280]{0:T(1024)}, u32[]{:S(2)}) copy-start(f32[1280]{0:T(1024)} %param.21) | copy-start | bytes 15364
  99.9 6.9 %copy-start.6 = (bf16[768,1280]{1,0:T(8,128)(2,1)S(1)}, bf16[768,1280]{1,0:T(8,128)(2,1)}, u32[]{:S(2)}) copy-start(bf16[768,1280]{1,0:T(8,128)(2,1)} %all-gather.5.cloned.1.call-done) | copy-start | bytes 5898244
  105.5 1.2 copy-start.8
  109.2 63.4 %reduce-scatter.3.cloned.1.call-start = ((), (), s32[]{:S(2)}) async-start(), calls=%async_computation.6 | async-start | bytes 2457600 | tf_op jit(solution)/shard_map/reduce_scatter | solution.py:99
  114.1 101.5 %reduce-scatter.5.cloned.1.call-start = ((), (), s32[]{:S(2)}) async-start(), calls=%async_computation.7 | async-start | bytes 2457600 | tf_op jit(solution)/shard_map/reduce_scatter | solution.py:102
  119.9 136.2 %all-reduce.8.cloned.1.call-start = ((), (), s32[]{:S(2)}) async-start(), calls=%async_computation.8 | async-start | bytes 1966080 | tf_op jit(solution)/shard_map/psum | solution.py:107
Sparse Core Ops, SparseCore 0:
  9.6 46.2 all-gather.4
  57.4 42.3 all-gather.2
  109.3 18.3 all-reduce.5
  130.0 42.6 reduce-scatter.2
  174.9 40.6 reduce-scatter.4
  218.0 38.0 all-reduce.7
where the time goes:
time: 268 us; the launch traced here: 267 us
  waiting for transfers between devices  151 us (56%)
  other arithmetic  63.8 us (24%)
  matrix products  23.4 us (9%)
  between operations  14.9 us (6%)
  local copies, waits for them, and re-layouts  6.86 us (3%)
  starting transfers between devices  6.85 us (3%)
    reduce_scatter x1, waiting for transfers between devices, on_device(): lax.psum_scatter(part_down.astype(jnp.bfloat16), 'seq', scatter_dimension...  43 us
    reduce_scatter x1, waiting for transfers between devices, on_device(): lax.psum_scatter(part_up.astype(jnp.bfloat16), 'seq', scatter_dimension=0...  39.7 us
    all_gather x1, waiting for transfers between devices, on_device(): lax.all_gather(w_down, 'seq', axis=0, tiled=True)  39 us
    convert_element_type x1, other arithmetic, on_device(): tile_grad = (out_grad + depthwise(conv_grad, flipped)).astype(jnp.bfloat16)  38.3 us
    all_gather x1, waiting for transfers between devices, on_device(): lax.all_gather(w_up, 'seq', axis=0, tiled=True)  18.1 us
    reduce_sum x1, other arithmetic, normalize(): center = jnp.mean(values, axis=-1, keepdims=True)  13 us
    psum x1, waiting for transfers between devices, on_device(): lax.psum(normed_part.astype(jnp.bfloat16), 'mp').astype(jnp.float32)  7.78 us
    all_to_all x1, starting transfers between devices, on_device(): lax.all_to_all(embed_grad[0], 'seq', split_axis=0, concat_axis=1, tiled=T...  6.46 us
  transfers between devices with their start and end apart: 7, of which 6 were waited for; matrix products, arithmetic and copies ran while one was open for 30% of the time, Pallas kernels for 0%

commit v1 on v0

--- a/solution.py
+++ b/solution.py
@@ -107,7 +107,9 @@
         lax.psum(up_piece.astype(jnp.bfloat16), "dp").astype(jnp.float32),
         lax.psum(down_piece.astype(jnp.bfloat16), "dp").astype(jnp.float32),
     )
-    normed_grad = lax.psum(normed_part.astype(jnp.bfloat16), "mp").astype(jnp.float32)
+    normed_grad = jnp.sum(lax.all_gather(normed_part.astype(jnp.bfloat16), "mp"), axis=0).astype(
+        jnp.float32
+    )
     conv_grad = norm_backward(normed_grad.reshape(conv.shape), normal, spread, ln_gain)
     tile_grad = (out_grad + depthwise(conv_grad, flipped)).astype(jnp.bfloat16)
     return (tile_grad, grad_up, grad_down)

time: 268 us -> 259 us (0.966)
  waiting for transfers between devices: 151 us -> 139 us
  other arithmetic: 63.8 us -> 67.4 us
    psum x1 -> x0, waiting for transfers between devices: 7.78 us -> none  [on_device(): lax.psum(normed_part.astype(jnp.bfloat16), 'mp').astype(jnp.float32)]
    convert_element_type x1, other arithmetic: 38.3 us -> 41.8 us  [on_device(): tile_grad = (out_grad + depthwise(conv_grad, flipped)).astype(jnp.bfloat16)]
  transfers between devices with their start and end apart: 7 -> 7, of which waited for: 6 -> 4; matrix products, arithmetic and copies ran while one was open for 30% -> 32% of each run, Pallas kernels for 0% -> 0%
where the time goes in v1:
time: 259 us; the launch traced here: 258 us
  waiting for transfers between devices  139 us (54%)
  other arithmetic  67.4 us (26%)
  matrix products  22.3 us (9%)
  between operations  15 us (6%)
  local copies, waits for them, and re-layouts  8.24 us (3%)
  starting transfers between devices  6.85 us (3%)
    reduce_scatter x1, waiting for transfers between devices, on_device(): lax.psum_scatter(part_down.astype(jnp.bfloat16), 'seq', scatter_dimension...  42.9 us
    convert_element_type x1, other arithmetic, on_device(): tile_grad = (out_grad + depthwise(conv_grad, flipped)).astype(jnp.bfloat16)  41.8 us
    all_gather x1, waiting for transfers between devices, on_device(): lax.all_gather(w_down, 'seq', axis=0, tiled=True)  38.9 us
    reduce_scatter x1, waiting for transfers between devices, on_device(): lax.psum_scatter(part_up.astype(jnp.bfloat16), 'seq', scatter_dimension=0...  37.3 us
    all_gather x1, waiting for transfers between devices, on_device(): lax.all_gather(w_up, 'seq', axis=0, tiled=True)  18 us
    reduce_sum x1, other arithmetic, normalize(): center = jnp.mean(values, axis=-1, keepdims=True)  13 us
    all_to_all x1, starting transfers between devices, on_device(): lax.all_to_all(embed_grad[0], 'seq', split_axis=0, concat_axis=1, tiled=T...  6.46 us
    dot_general x1, matrix products, on_device(): lax.dot_general(branch_grad, act, (((0,), (0,)), ((), ())), preferred_ele...  5.43 us
  transfers between devices with their start and end apart: 7, of which 4 were waited for; matrix products, arithmetic and copies ran while one was open for 32% of the time, Pallas kernels for 0%

profile of v1, /device:TPU:0, one launch (start us, length us, event | category | flops | bytes accessed | tf_op | source)
XLA Modules:
  0.0 258.3 jit_solution(2462999262779796685)
XLA Ops:
  7.2 0.0 all-gather.7.cloned.1.call-start
  7.2 0.7 all-gather.7.cloned.1.call-update
  7.9 0.7 all_to_all.10
  8.7 0.7 reshape.225
  9.4 6.5 %all-to-all-start = ((bf16[4,2,960]{2,1,0:T(2,128)(2,1)}), bf16[4,2,960]{2,1,0:T(2,128)(2,1)S(1)}, u32[]{:S(2)}, u32[]{:S(2)}) async-start(bf16[4,2,960]{2,1,0:T(2,128)(2,1)} %reshape.225), calls=%async_computation | async-start | bytes 32768 | tf_op jit(solution)/shard_map/all_to_all | solution.py:72
  15.8 0.7 all-gather.5.cloned.1.call-update
  16.6 0.0 all-gather.9.cloned.1.call-start
  16.6 1.1 slice_reduce_fusion.46
  17.7 1.5 slice_reduce_fusion.48
  19.2 1.4 slice_reduce_fusion.47
  20.6 0.2 convert_element_type.79
  20.8 13.0 %fusion.209 = (f32[10,8,8]{2,1,0:T(8,128)S(1)}, f32[10,8,8,768]{3,2,1,0:T(8,128)S(1)}) fusion(f32[768]{0:T(1024)S(1)} %copy-done.9, f32[768]{0:T(1024)S(1)} %get-tuple-element.50, f32[768]{0:T(1024)S(1)} %get-tuple-element.51, f32[768]{0:T(1024)S(1)} %get-tuple-element.4, f32[768]{0:T(1024)S(1)} %get-tuple-element.5, f32[768]{0:T(1024)S(1)} %get-tuple-element.6, ...), kind=kLoop, calls=%fused_computation.377 | loop fusion | flops 48659840 | bytes 4088320 | tf_op jit(solution)/shard_map/reduce_sum | solution.py:39
  34.5 0.3 multiply_reduce_fusion.2
  34.8 0.0 copy-start
  34.8 0.0 copy-start.8
  34.9 1.3 add_convert_fusion
  36.2 0.1 reshape.226
  36.4 0.1 reshape.173
  36.5 0.1 multiply_multiply_fusion.1
  36.6 1.3 multiply_convert_fusion.1
  37.9 18.0 %all-gather.7.cloned.1.call-done = bf16[768,1280]{1,0:T(8,128)(2,1)} async-done(((bf16[192,1280]{1,0:T(8,128)(2,1)}), bf16[768,1280]{1,0:T(8,128)(2,1)}) %all-gather.7.cloned.1.call-update) | async-done | bytes 1966096 | tf_op jit(solution)/shard_map/all_gather | solution.py:82
  55.9 5.1 %convolution_add_fusion = f32[640,1280]{1,0:T(8,128)} fusion(bf16[640,768]{1,0:T(8,128)(2,1)} %bitcast.20, bf16[768,1280]{1,0:T(8,128)(2,1)} %all-gather.7.cloned.1.call-done, f32[1280]{0:T(1024)S(1)} %copy-done.11), kind=kOutput, calls=%fused_computation.99 | convolution fusion | flops 1259110400 | bytes 6231040 | tf_op jit(solution)/shard_map/dot_general | solution.py:85
  60.9 38.9 %all-gather.5.cloned.1.call-done = bf16[768,1280]{1,0:T(8,128)(2,1)} async-done(((bf16[192,1280]{1,0:T(8,128)(2,1)}), bf16[768,1280]{1,0:T(8,128)(2,1)}) %all-gather.5.cloned.1.call-update) | async-done | bytes 1966096 | tf_op jit(solution)/shard_map/all_gather | solution.py:83
  99.9 4.9 %fusion.5 = bf16[640,1280]{1,0:T(8,128)(2,1)S(1)} fusion(f32[640,1280]{1,0:T(8,128)} %convolution_add_fusion, bf16[640,768]{1,0:T(8,128)(2,1)S(1)} %bitcast.22, bf16[768,1280]{1,0:T(8,128)(2,1)} %all-gather.5.cloned.1.call-done), kind=kOutput, calls=%fused_computation.108 | convolution fusion | flops 1273856000 | bytes 7864320 | tf_op jit(solution)/shard_map/dot_general | solution.py:87
  104.8 1.2 copy-done.12
  106.0 2.4 convolution_convert_fusion.2
  108.4 0.0 all-gather.9.cloned.1.call-update
  108.5 0.0 reduce-scatter.3.cloned.1.call-start
  108.5 4.5 %convolution_convert_fusion.1 = bf16[768,1280]{1,0:T(8,128)(2,1)} fusion(bf16[640,768]{1,0:T(8,128)(2,1)S(1)} %bitcast.21, bf16[640,1280]{1,0:T(8,128)(2,1)} %copy-done.12), kind=kOutput, calls=%fused_computation.101 | convolution fusion | flops 1259274240 | bytes 4587520 | tf_op jit(solution)/shard_map/dot_general | solution.py:95
  113.0 0.0 reduce-scatter.3.cloned.1.call-update
  113.0 0.0 reduce-scatter.5.cloned.1.call-start
  113.1 1.2 copy-done.5
  114.3 5.4 %convolution_convert_fusion = bf16[768,1280]{1,0:T(8,128)(2,1)} fusion(bf16[640,768]{1,0:T(8,128)(2,1)S(1)} %bitcast.23, f32[640,1280]{1,0:T(8,128)} %convolution_add_fusion), kind=kOutput, calls=%fused_computation.100 | convolution fusion | flops 1266647040 | bytes 6225920 | tf_op jit(solution)/shard_map/dot_general | solution.py:92
  119.7 0.0 reduce-scatter.5.cloned.1.call-update
  119.8 0.2 all-reduce.5.cloned.1.call-start
  120.0 0.0 all-gather.9.cloned.1.call-done
  120.0 2.5 reduce_sum.50
  122.5 0.3 multiply_reduce_fusion.1
  122.8 0.1 div.41
  122.8 0.6 multiply_reduce_fusion
  123.5 1.9 subtract_divide_fusion
  125.4 37.3 %reduce-scatter.3.cloned.1.call-done = bf16[192,1280]{1,0:T(8,128)(2,1)} async-done(((bf16[768,1280]{1,0:T(8,128)(2,1)}), bf16[192,1280]{1,0:T(8,128)(2,1)}) %reduce-scatter.3.cloned.1.call-update) | async-done | bytes 491536 | tf_op jit(solution)/shard_map/reduce_scatter | solution.py:99
  162.7 42.9 %reduce-scatter.5.cloned.1.call-done = bf16[192,1280]{1,0:T(8,128)(2,1)} async-done(((bf16[768,1280]{1,0:T(8,128)(2,1)}), bf16[192,1280]{1,0:T(8,128)(2,1)}) %reduce-scatter.5.cloned.1.call-update) | async-done | bytes 491536 | tf_op jit(solution)/shard_map/reduce_scatter | solution.py:102
  205.5 0.0 all-reduce.5.cloned.1.call-update
  205.6 41.8 %fusion.200 = bf16[10,8,8,768]{3,2,1,0:T(8,128)(2,1)} fusion(f32[10,8,8,768]{3,2,1,0:T(8,128)} %subtract_divide_fusion, bf16[10,8,8,768]{3,2,1,0:T(8,128)(2,1)S(1)} %copy-done.1, f32[768]{0:T(1024)S(1)} %get-tuple-element.50, f32[768]{0:T(1024)S(1)} %get-tuple-element.51, f32[768]{0:T(1024)S(1)} %get-tuple-element.4, f32[768]{0:T(1024)S(1)} %get-tuple-element.5, ...), kind=kLoop, calls=%fused_computation.310 | loop fusion | flops 50135040 | bytes 4113448 | tf_op jit(solution)/shard_map/convert_element_type | solution.py:114
  247.3 0.0 all-reduce.5.cloned.1.call-done
  247.4 2.0 convert_element_type.88
  249.4 2.0 convert_element_type.91
  (31 shorter events, 0.1 us)
Async XLA Ops:
  7.2 13.4 %copy-start.2 = (bf16[10,8,8,768]{3,2,1,0:T(8,128)(2,1)S(1)}, bf16[10,8,8,768]{3,2,1,0:T(8,128)(2,1)}, u32[]{:S(2)}) copy-start(bf16[10,8,8,768]{3,2,1,0:T(8,128)(2,1)} %param.12) | copy-start | bytes 2949124
  7.2 48.7 %all-gather.7.cloned.1.call-start = ((), (), s32[]{:S(2)}) async-start(), calls=%async_computation.4 | async-start | bytes 2457600 | tf_op jit(solution)/shard_map/all_gather | solution.py:82
  9.4 11.4 %copy-start.9 = (f32[768]{0:T(1024)S(1)}, f32[768]{0:T(1024)}, u32[]{:S(2)}) copy-start(f32[768]{0:T(1024)} %param.17) | copy-start | bytes 9220
  9.4 26.9 %all-to-all-start = ((bf16[4,2,960]{2,1,0:T(2,128)(2,1)}), bf16[4,2,960]{2,1,0:T(2,128)(2,1)S(1)}, u32[]{:S(2)}, u32[]{:S(2)}) async-start(bf16[4,2,960]{2,1,0:T(2,128)(2,1)} %reshape.225), calls=%async_computation | async-start | bytes 32768 | tf_op jit(solution)/shard_map/all_to_all | solution.py:72
  15.8 84.0 %all-gather.5.cloned.1.call-start = ((), (), s32[]{:S(2)}) async-start(), calls=%async_computation.3 | async-start | bytes 2457600 | tf_op jit(solution)/shard_map/all_gather | solution.py:83
  16.6 103.5 %all-gather.9.cloned.1.call-start = ((), (), s32[]{:S(2)}) async-start(), calls=%async_computation.7 | async-start | bytes 2949120 | tf_op jit(solution)/shard_map/all_gather | solution.py:110
  33.8 1.1 copy-start.6
  33.8 1.1 copy-start.7
  34.8 1.7 copy-start
  34.8 1.7 copy-start.8
  36.2 19.7 %copy-start.11 = (f32[1280]{0:T(1024)S(1)}, f32[1280]{0:T(1024)}, u32[]{:S(2)}) copy-start(f32[1280]{0:T(1024)} %param.21) | copy-start | bytes 15364
  55.9 44.0 %copy-start.4 = (bf16[10,8,8,768]{3,2,1,0:T(8,128)(2,1)S(1)}, bf16[10,8,8,768]{3,2,1,0:T(8,128)(2,1)}, u32[]{:S(2)}) copy-start(bf16[10,8,8,768]{3,2,1,0:T(8,128)(2,1)} %multiply_convert_fusion.1) | copy-start | bytes 2949124
  99.9 6.1 %copy-start.10 = (bf16[768,1280]{1,0:T(8,128)(2,1)S(1)}, bf16[768,1280]{1,0:T(8,128)(2,1)}, u32[]{:S(2)}) copy-start(bf16[768,1280]{1,0:T(8,128)(2,1)} %all-gather.7.cloned.1.call-done) | copy-start | bytes 5898244
  104.8 1.3 copy-start.12
  106.0 2.5 copy-start.3
  108.5 54.2 %reduce-scatter.3.cloned.1.call-start = ((), (), s32[]{:S(2)}) async-start(), calls=%async_computation.5 | async-start | bytes 2457600 | tf_op jit(solution)/shard_map/reduce_scatter | solution.py:99
  113.0 1.3 copy-start.5
  113.0 92.5 %reduce-scatter.5.cloned.1.call-start = ((), (), s32[]{:S(2)}) async-start(), calls=%async_computation.6 | async-start | bytes 2457600 | tf_op jit(solution)/shard_map/reduce_scatter | solution.py:102
  119.8 127.6 %all-reduce.5.cloned.1.call-start = ((), (), s32[]{:S(2)}) async-start(), calls=%async_computation.8 | async-start | bytes 1966080 | tf_op jit(solution)/shard_map/psum | solution.py:107
  123.5 82.1 %copy-start.1 = (bf16[10,8,8,768]{3,2,1,0:T(8,128)(2,1)S(1)}, bf16[10,8,8,768]{3,2,1,0:T(8,128)(2,1)}, u32[]{:S(2)}) copy-start(bf16[10,8,8,768]{3,2,1,0:T(8,128)(2,1)} %param.13) | copy-start | bytes 2949124
Sparse Core Ops, SparseCore 0:
  9.6 46.2 all-gather.6
  57.4 42.3 all-gather.4
  108.6 9.2 all-gather.8
  120.0 42.6 reduce-scatter.2
  164.8 40.6 reduce-scatter.4
  207.8 37.9 all-reduce.4
